TPU v7x, 32 devices: a whole 2x2x4 slice. The times are simulated.
32 devices in a mesh: twin: 2 (over core), dp: 4 (over y, x), fsdp: 4 (over z).
Axes of the slice: x: 2, y: 2, z: 4, core: 2. Of those that a mesh axis runs over, the one named last changes fastest.
Arguments:
- tokens: bfloat16 [64, 512, 768], P(('twin', 'dp', 'fsdp')), may hold values from -6 to 6
- w_query: bfloat16 [768, 768], P('fsdp'), may hold values from -0.21875 to 0.21875
- b_query: bfloat16 [768], P('fsdp'), may hold values from -3 to 3
- w_key: bfloat16 [768, 768], P('fsdp'), may hold values from -0.21875 to 0.21875
- w_value: bfloat16 [768, 768], P('fsdp'), may hold values from -0.21875 to 0.21875
- b_value: bfloat16 [768], P('fsdp'), may hold values from -3 to 3
- w_out: bfloat16 [768, 768], P('fsdp'), may hold values from -0.875 to 0.875
- b_out: bfloat16 [768], P('fsdp'), may hold values from -3 to 3
- gain_attn: bfloat16 [768], P('fsdp'), may hold values from 0.5 to 1.5
- shift_attn: bfloat16 [768], P('fsdp'), may hold values from -2 to 2
- w_inner: bfloat16 [768, 3072], P('fsdp'), may hold values from -0.21875 to 0.21875
- b_inner: bfloat16 [3072], P('fsdp'), may hold values from -3 to 3
- w_outer: bfloat16 [3072, 768], P('fsdp'), may hold values from -0.109375 to 0.109375
- b_outer: bfloat16 [768], P('fsdp'), may hold values from -3 to 3
- gain_ffn: bfloat16 [768], P('fsdp'), may hold values from 0.5 to 1.5
- shift_ffn: bfloat16 [768], P('fsdp'), may hold values from -0.59765625 to 0.59765625
- lengths: int32 [64, 9], P(('twin', 'dp', 'fsdp')), may hold values from 1 to 128, 512 in all within a row
- labels: int32 [256], replicated, may hold values from 0 to 255, each once
Outputs:
- output: bfloat16 [64, 512, 768], P(('twin', 'dp', 'fsdp'))
- grad_tokens: bfloat16 [64, 512, 768], P(('twin', 'dp', 'fsdp'))
- grad_w_query: float32 [768, 768], P('fsdp')
- grad_b_query: float32 [768], P('fsdp')
- grad_w_key: float32 [768, 768], P('fsdp')
- grad_w_value: float32 [768, 768], P('fsdp')
- grad_b_value: float32 [768], P('fsdp')
- grad_w_out: float32 [768, 768], P('fsdp')
- grad_b_out: float32 [768], P('fsdp')
- grad_gain_attn: float32 [768], P('fsdp')
- grad_shift_attn: float32 [768], P('fsdp')
- grad_w_inner: float32 [768, 3072], P('fsdp')
- grad_b_inner: float32 [3072], P('fsdp')
- grad_w_outer: float32 [3072, 768], P('fsdp')
- grad_b_outer: float32 [768], P('fsdp')
- grad_gain_ffn: float32 [768], P('fsdp')
- grad_shift_ffn: float32 [768], P('fsdp')
Inputs may be any that keep to these rules, and one draw needn't show every extreme that they name: `lengths`: each row's first 8 entries are the token counts of its sentences in order and the last is the count of its padding tokens; the entries of a row sum to 512. labels[i] is the positive sentence paired with anchor i; every positive is named by exactly one anchor.
All inputs are finite; a program needn't handle non-finite values.
Results may differ from a plain program's by a relative error of at most 0.02.
Values may be sent and summed in bfloat16 or wider, within the bound.
No kernel may reach another device: no remote copies, remote signals or barrier semaphores. Data moves between devices by JAX's collectives and lax.ppermute only.
A program may use at most 192 MiB of HBM per device.

v0:
```python
import jax
import jax.numpy as jnp
from jax import lax
from jax.sharding import PartitionSpec as P

H = 12
HD = 64
SEG = 8
MB = 2


norm_eps = 1e-12
pool_eps = 1e-06
sim_scale = 20.0


def cross_dot(left, right):
    return lax.dot_general(
        left, right, (((0,), (0,)), ((), ())), preferred_element_type=jnp.float32
    )


def back_dot(left, right):
    return lax.dot_general(
        left, right, (((1,), (1,)), ((), ())), preferred_element_type=jnp.float32
    )


def plain_dot(left, right):
    return jnp.dot(left, right, preferred_element_type=jnp.float32)


def segment_ids(lengths, seq_len):
    ends = jnp.cumsum(lengths, axis=1, dtype=jnp.int32)
    position = jnp.arange(seq_len, dtype=jnp.int32)
    return jnp.sum((position[None, :, None] >= ends[:, None, :]).astype(jnp.int32), axis=2)


def normalize(hidden):
    centred = hidden - jnp.mean(hidden, axis=-1, keepdims=True)
    inv_dev = lax.rsqrt(jnp.mean(centred * centred, axis=-1, keepdims=True) + norm_eps)
    return (centred * inv_dev, inv_dev)


def norm_back(grad_normed, normed, inv_dev):
    return inv_dev * (
        grad_normed
        - jnp.mean(grad_normed, axis=-1, keepdims=True)
        - normed * jnp.mean(grad_normed * normed, axis=-1, keepdims=True)
    )


def gelu_parts(inner):
    cdf_value = 0.5 * (1.0 + lax.erf(inner * 0.7071067811865476))
    slope = cdf_value + inner * jnp.exp(-0.5 * inner * inner) * 0.3989422804014327
    return (cdf_value, slope)


def masked_scores(query, keys, seg_row):
    scores = jnp.einsum("qhd,khd->hqk", query, keys, preferred_element_type=jnp.float32) * HD ** (
        -0.5
    )
    same = seg_row[:, None] == seg_row[None, :]
    return jnp.where(same[None], scores, -1e30)


def attend(item):
    query, keys, values, seg_row = item
    scores = masked_scores(query, keys, seg_row)
    row_max = jnp.max(scores, axis=2, keepdims=True)
    exp_scores = jnp.exp(scores - row_max)
    row_sum = jnp.sum(exp_scores, axis=2, keepdims=True)
    attn_prob = (exp_scores / row_sum).astype(jnp.bfloat16)
    context = jnp.einsum("hqk,khd->qhd", attn_prob, values, preferred_element_type=jnp.float32)
    return (context.astype(jnp.bfloat16), row_max[:, :, 0] + jnp.log(row_sum[:, :, 0]))


def attend_back(item):
    query, keys, values, seg_row, log_total, grad_ctx = item
    attn_prob = jnp.exp(masked_scores(query, keys, seg_row) - log_total[:, :, None])
    grad_values = jnp.einsum(
        "hqk,qhd->khd", attn_prob.astype(jnp.bfloat16), grad_ctx, preferred_element_type=jnp.float32
    )
    grad_prob = jnp.einsum("qhd,khd->hqk", grad_ctx, values, preferred_element_type=jnp.float32)
    grad_scores = attn_prob * (grad_prob - jnp.sum(attn_prob * grad_prob, axis=2, keepdims=True))
    grad_scores = grad_scores.astype(jnp.bfloat16)
    grad_query = jnp.einsum(
        "hqk,khd->qhd", grad_scores, keys, preferred_element_type=jnp.float32
    ) * HD ** (-0.5)
    grad_keys = jnp.einsum(
        "hqk,qhd->khd", grad_scores, query, preferred_element_type=jnp.float32
    ) * HD ** (-0.5)
    return (
        grad_query.astype(jnp.bfloat16),
        grad_keys.astype(jnp.bfloat16),
        grad_values.astype(jnp.bfloat16),
    )


def forward_block(block_tok, seg_block, weights):
    (
        w_query,
        b_query,
        w_key,
        w_value,
        b_value,
        w_out,
        b_out,
        gain_attn,
        shift_attn,
        w_inner,
        b_inner,
        w_outer,
        b_outer,
        gain_ffn,
        shift_ffn,
    ) = weights
    row_count, seq_len, model_dim = block_tok.shape
    tok_flat = block_tok.reshape(row_count * seq_len, model_dim)
    head_shape = (row_count, seq_len, H, HD)
    query = (plain_dot(tok_flat, w_query) + b_query).astype(jnp.bfloat16).reshape(head_shape)
    keys = plain_dot(tok_flat, w_key).astype(jnp.bfloat16).reshape(head_shape)
    values = (plain_dot(tok_flat, w_value) + b_value).astype(jnp.bfloat16).reshape(head_shape)
    context, log_total = lax.map(attend, (query, keys, values, seg_block))
    context = context.reshape(row_count * seq_len, model_dim)
    normed_attn, inv_attn = normalize(
        tok_flat.astype(jnp.float32) + plain_dot(context, w_out) + b_out
    )
    mid_state = normed_attn * gain_attn + shift_attn
    mid_low = mid_state.astype(jnp.bfloat16)
    inner = plain_dot(mid_low, w_inner) + b_inner
    cdf_value, slope = gelu_parts(inner)
    activ = (inner * cdf_value).astype(jnp.bfloat16)
    normed_ffn, inv_ffn = normalize(mid_state + plain_dot(activ, w_outer) + b_outer)
    final = normed_ffn * gain_ffn + shift_ffn
    saved = (
        query,
        keys,
        values,
        log_total,
        context,
        normed_attn,
        inv_attn,
        mid_low,
        inner,
        activ,
        normed_ffn,
        inv_ffn,
    )
    return (final, saved)


def backward_block(grad_final, block_tok, seg_block, weights, saved):
    (
        w_query,
        b_query,
        w_key,
        w_value,
        b_value,
        w_out,
        b_out,
        gain_attn,
        shift_attn,
        w_inner,
        b_inner,
        w_outer,
        b_outer,
        gain_ffn,
        shift_ffn,
    ) = weights
    (
        query,
        keys,
        values,
        log_total,
        context,
        normed_attn,
        inv_attn,
        mid_low,
        inner,
        activ,
        normed_ffn,
        inv_ffn,
    ) = saved
    row_count, seq_len, model_dim = block_tok.shape
    tok_flat = block_tok.reshape(row_count * seq_len, model_dim)
    grad_gain_ffn = jnp.sum(grad_final * normed_ffn, axis=0)
    grad_shift_ffn = jnp.sum(grad_final, axis=0)
    grad_h2 = norm_back(grad_final * gain_ffn, normed_ffn, inv_ffn)
    grad_branch = grad_h2.astype(jnp.bfloat16)
    grad_w_outer = cross_dot(activ, grad_branch)
    grad_b_outer = jnp.sum(grad_branch, axis=0, dtype=jnp.float32)
    cdf_value, slope = gelu_parts(inner)
    grad_inner = (back_dot(grad_branch, w_outer) * slope).astype(jnp.bfloat16)
    grad_w_inner = cross_dot(mid_low, grad_inner)
    grad_b_inner = jnp.sum(grad_inner, axis=0, dtype=jnp.float32)
    grad_mid = grad_h2 + back_dot(grad_inner, w_inner)
    grad_gain_attn = jnp.sum(grad_mid * normed_attn, axis=0)
    grad_shift_attn = jnp.sum(grad_mid, axis=0)
    grad_h1 = norm_back(grad_mid * gain_attn, normed_attn, inv_attn)
    grad_attn = grad_h1.astype(jnp.bfloat16)
    grad_w_out = cross_dot(context, grad_attn)
    grad_b_out = jnp.sum(grad_attn, axis=0, dtype=jnp.float32)
    grad_ctx = back_dot(grad_attn, w_out).astype(jnp.bfloat16).reshape(row_count, seq_len, H, HD)
    grad_query, grad_keys, grad_values = lax.map(
        attend_back, (query, keys, values, seg_block, log_total, grad_ctx)
    )
    flat_shape = (row_count * seq_len, model_dim)
    grad_query = grad_query.reshape(flat_shape)
    grad_keys = grad_keys.reshape(flat_shape)
    grad_values = grad_values.reshape(flat_shape)
    grad_w_query = cross_dot(tok_flat, grad_query)
    grad_b_query = jnp.sum(grad_query, axis=0, dtype=jnp.float32)
    grad_w_key = cross_dot(tok_flat, grad_keys)
    grad_w_value = cross_dot(tok_flat, grad_values)
    grad_b_value = jnp.sum(grad_values, axis=0, dtype=jnp.float32)
    grad_tok = (
        grad_h1
        + back_dot(grad_query, w_query)
        + back_dot(grad_keys, w_key)
        + back_dot(grad_values, w_value)
    )
    grads = (
        grad_w_query,
        grad_b_query,
        grad_w_key,
        grad_w_value,
        grad_b_value,
        grad_w_out,
        grad_b_out,
        grad_gain_attn,
        grad_shift_attn,
        grad_w_inner,
        grad_b_inner,
        grad_w_outer,
        grad_b_outer,
        grad_gain_ffn,
        grad_shift_ffn,
    )
    return (grad_tok.astype(jnp.bfloat16).reshape(row_count, seq_len, model_dim), grads)


def reduce_grads(grads):
    (
        grad_w_query,
        grad_b_query,
        grad_w_key,
        grad_w_value,
        grad_b_value,
        grad_w_out,
        grad_b_out,
        grad_gain_attn,
        grad_shift_attn,
        grad_w_inner,
        grad_b_inner,
        grad_w_outer,
        grad_b_outer,
        grad_gain_ffn,
        grad_shift_ffn,
    ) = grads
    (
        shard_w_query,
        shard_b_query,
        shard_w_key,
        shard_w_value,
        shard_b_value,
        shard_w_out,
        shard_b_out,
        shard_gain_attn,
        shard_shift_attn,
        shard_w_inner,
        shard_b_inner,
        shard_w_outer,
        shard_b_outer,
        shard_gain_ffn,
        shard_shift_ffn,
    ) = (
        lax.psum_scatter(
            grad_w_query.astype(jnp.bfloat16), "fsdp", scatter_dimension=0, tiled=True
        ).astype(jnp.float32),
        lax.psum_scatter(
            grad_b_query.astype(jnp.bfloat16), "fsdp", scatter_dimension=0, tiled=True
        ).astype(jnp.float32),
        lax.psum_scatter(
            grad_w_key.astype(jnp.bfloat16), "fsdp", scatter_dimension=0, tiled=True
        ).astype(jnp.float32),
        lax.psum_scatter(
            grad_w_value.astype(jnp.bfloat16), "fsdp", scatter_dimension=0, tiled=True
        ).astype(jnp.float32),
        lax.psum_scatter(
            grad_b_value.astype(jnp.bfloat16), "fsdp", scatter_dimension=0, tiled=True
        ).astype(jnp.float32),
        lax.psum_scatter(
            grad_w_out.astype(jnp.bfloat16), "fsdp", scatter_dimension=0, tiled=True
        ).astype(jnp.float32),
        lax.psum_scatter(
            grad_b_out.astype(jnp.bfloat16), "fsdp", scatter_dimension=0, tiled=True
        ).astype(jnp.float32),
        lax.psum_scatter(
            grad_gain_attn.astype(jnp.bfloat16), "fsdp", scatter_dimension=0, tiled=True
        ).astype(jnp.float32),
        lax.psum_scatter(
            grad_shift_attn.astype(jnp.bfloat16), "fsdp", scatter_dimension=0, tiled=True
        ).astype(jnp.float32),
        lax.psum_scatter(
            grad_w_inner.astype(jnp.bfloat16), "fsdp", scatter_dimension=0, tiled=True
        ).astype(jnp.float32),
        lax.psum_scatter(
            grad_b_inner.astype(jnp.bfloat16), "fsdp", scatter_dimension=0, tiled=True
        ).astype(jnp.float32),
        lax.psum_scatter(
            grad_w_outer.astype(jnp.bfloat16), "fsdp", scatter_dimension=0, tiled=True
        ).astype(jnp.float32),
        lax.psum_scatter(
            grad_b_outer.astype(jnp.bfloat16), "fsdp", scatter_dimension=0, tiled=True
        ).astype(jnp.float32),
        lax.psum_scatter(
            grad_gain_ffn.astype(jnp.bfloat16), "fsdp", scatter_dimension=0, tiled=True
        ).astype(jnp.float32),
        lax.psum_scatter(
            grad_shift_ffn.astype(jnp.bfloat16), "fsdp", scatter_dimension=0, tiled=True
        ).astype(jnp.float32),
    )
    return (
        lax.psum(shard_w_query.astype(jnp.bfloat16), ("twin", "dp")).astype(jnp.float32),
        lax.psum(shard_b_query.astype(jnp.bfloat16), ("twin", "dp")).astype(jnp.float32),
        lax.psum(shard_w_key.astype(jnp.bfloat16), ("twin", "dp")).astype(jnp.float32),
        lax.psum(shard_w_value.astype(jnp.bfloat16), ("twin", "dp")).astype(jnp.float32),
        lax.psum(shard_b_value.astype(jnp.bfloat16), ("twin", "dp")).astype(jnp.float32),
        lax.psum(shard_w_out.astype(jnp.bfloat16), ("twin", "dp")).astype(jnp.float32),
        lax.psum(shard_b_out.astype(jnp.bfloat16), ("twin", "dp")).astype(jnp.float32),
        lax.psum(shard_gain_attn.astype(jnp.bfloat16), ("twin", "dp")).astype(jnp.float32),
        lax.psum(shard_shift_attn.astype(jnp.bfloat16), ("twin", "dp")).astype(jnp.float32),
        lax.psum(shard_w_inner.astype(jnp.bfloat16), ("twin", "dp")).astype(jnp.float32),
        lax.psum(shard_b_inner.astype(jnp.bfloat16), ("twin", "dp")).astype(jnp.float32),
        lax.psum(shard_w_outer.astype(jnp.bfloat16), ("twin", "dp")).astype(jnp.float32),
        lax.psum(shard_b_outer.astype(jnp.bfloat16), ("twin", "dp")).astype(jnp.float32),
        lax.psum(shard_gain_ffn.astype(jnp.bfloat16), ("twin", "dp")).astype(jnp.float32),
        lax.psum(shard_shift_ffn.astype(jnp.bfloat16), ("twin", "dp")).astype(jnp.float32),
    )


def per_device(
    tokens,
    w_query,
    b_query,
    w_key,
    w_value,
    b_value,
    w_out,
    b_out,
    gain_attn,
    shift_attn,
    w_inner,
    b_inner,
    w_outer,
    b_outer,
    gain_ffn,
    shift_ffn,
    lengths,
    labels,
):
    row_total, seq_len, model_dim = tokens.shape
    block_rows = row_total // MB
    seg_all = segment_ids(lengths, seq_len)
    member = (seg_all[:, None, :] == jnp.arange(SEG, dtype=jnp.int32)[None, :, None]).astype(
        jnp.float32
    )
    counts = lengths[:, :SEG].astype(jnp.float32)
    finals = []
    saved_list = []
    for block_idx in range(MB):
        row_span = slice(block_idx * block_rows, (block_idx + 1) * block_rows)
        weights = (
            lax.all_gather(w_query, "fsdp", axis=0, tiled=True),
            lax.all_gather(b_query, "fsdp", axis=0, tiled=True),
            lax.all_gather(w_key, "fsdp", axis=0, tiled=True),
            lax.all_gather(w_value, "fsdp", axis=0, tiled=True),
            lax.all_gather(b_value, "fsdp", axis=0, tiled=True),
            lax.all_gather(w_out, "fsdp", axis=0, tiled=True),
            lax.all_gather(b_out, "fsdp", axis=0, tiled=True),
            lax.all_gather(gain_attn, "fsdp", axis=0, tiled=True),
            lax.all_gather(shift_attn, "fsdp", axis=0, tiled=True),
            lax.all_gather(w_inner, "fsdp", axis=0, tiled=True),
            lax.all_gather(b_inner, "fsdp", axis=0, tiled=True),
            lax.all_gather(w_outer, "fsdp", axis=0, tiled=True),
            lax.all_gather(b_outer, "fsdp", axis=0, tiled=True),
            lax.all_gather(gain_ffn, "fsdp", axis=0, tiled=True),
            lax.all_gather(shift_ffn, "fsdp", axis=0, tiled=True),
        )
        final, saved = forward_block(tokens[row_span], seg_all[row_span], weights)
        finals.append(final.reshape(block_rows, seq_len, model_dim))
        saved_list.append(saved)
    final_all = jnp.concatenate(finals, axis=0)
    pooled_f = (
        jnp.einsum("rst,rtd->rsd", member, final_all, precision=lax.Precision.HIGHEST)
        / counts[:, :, None]
    )
    pooled_low = pooled_f.reshape(row_total * SEG, model_dim).astype(jnp.bfloat16)
    gathered = lax.all_gather(pooled_low, ("twin", "dp", "fsdp"), axis=0, tiled=True)
    own_count = pooled_low.shape[0]
    half_count = labels.shape[0]
    twin_side = lax.axis_index("twin")
    device = lax.axis_index(("twin", "dp", "fsdp"))
    first_seg = device * own_count
    other_start = (1 - twin_side) * half_count
    other_side = lax.dynamic_slice_in_dim(gathered, other_start, half_count, 0)
    own_f = pooled_low.astype(jnp.float32)
    other_f = other_side.astype(jnp.float32)
    inv_own = lax.rsqrt(jnp.sum(own_f * own_f, axis=1) + pool_eps)
    inv_other = lax.rsqrt(jnp.sum(other_f * other_f, axis=1) + pool_eps)
    col_index = jnp.arange(half_count, dtype=jnp.int32)
    similar = sim_scale * back_dot(pooled_low, other_side) * inv_own[:, None] * inv_other[None, :]
    own_labels = lax.dynamic_slice_in_dim(
        labels, jnp.minimum(first_seg, half_count - own_count), own_count, 0
    )
    own_index = first_seg - half_count + jnp.arange(own_count, dtype=jnp.int32)
    target = jnp.where(
        twin_side == 0,
        col_index[None, :] == own_labels[:, None],
        labels[None, :] == own_index[:, None],
    ).astype(jnp.float32)
    row_max = jnp.max(similar, axis=1, keepdims=True)
    log_total = row_max[:, 0] + jnp.log(jnp.sum(jnp.exp(similar - row_max), axis=1))
    grad_sim = jnp.exp(similar - log_total[:, None]) - target
    weighted = grad_sim * similar
    grad_raw = sim_scale * grad_sim * inv_own[:, None] * inv_other[None, :]
    grad_own = (
        jnp.dot(grad_raw, other_f, precision=lax.Precision.HIGHEST)
        - (jnp.sum(weighted, axis=1) * inv_own * inv_own)[:, None] * own_f
    )
    grad_other = (
        lax.dot_general(grad_raw, own_f, (((0,), (0,)), ((), ())), precision=lax.Precision.HIGHEST)
        - (jnp.sum(weighted, axis=0) * inv_other * inv_other)[:, None] * other_f
    )
    term = jnp.zeros((2 * half_count, model_dim), jnp.float32)
    term = lax.dynamic_update_slice_in_dim(term, grad_other, other_start, 0)
    term = lax.dynamic_update_slice_in_dim(term, grad_own, first_seg, 0)
    grad_pooled = lax.psum_scatter(term, ("twin", "dp", "fsdp"), scatter_dimension=0, tiled=True)
    grad_scaled = grad_pooled.reshape(row_total, SEG, model_dim) / counts[:, :, None]
    grad_toks = []
    grad_total = None
    for block_idx in range(MB):
        row_span = slice(block_idx * block_rows, (block_idx + 1) * block_rows)
        weights = (
            lax.all_gather(w_query, "fsdp", axis=0, tiled=True),
            lax.all_gather(b_query, "fsdp", axis=0, tiled=True),
            lax.all_gather(w_key, "fsdp", axis=0, tiled=True),
            lax.all_gather(w_value, "fsdp", axis=0, tiled=True),
            lax.all_gather(b_value, "fsdp", axis=0, tiled=True),
            lax.all_gather(w_out, "fsdp", axis=0, tiled=True),
            lax.all_gather(b_out, "fsdp", axis=0, tiled=True),
            lax.all_gather(gain_attn, "fsdp", axis=0, tiled=True),
            lax.all_gather(shift_attn, "fsdp", axis=0, tiled=True),
            lax.all_gather(w_inner, "fsdp", axis=0, tiled=True),
            lax.all_gather(b_inner, "fsdp", axis=0, tiled=True),
            lax.all_gather(w_outer, "fsdp", axis=0, tiled=True),
            lax.all_gather(b_outer, "fsdp", axis=0, tiled=True),
            lax.all_gather(gain_ffn, "fsdp", axis=0, tiled=True),
            lax.all_gather(shift_ffn, "fsdp", axis=0, tiled=True),
        )
        grad_final = jnp.einsum(
            "rst,rsd->rtd", member[row_span], grad_scaled[row_span], precision=lax.Precision.HIGHEST
        ).reshape(block_rows * seq_len, model_dim)
        grad_tok, grads = backward_block(
            grad_final, tokens[row_span], seg_all[row_span], weights, saved_list[block_idx]
        )
        grad_toks.append(grad_tok)
        grads = reduce_grads(grads)
        grad_total = grads if grad_total is None else jax.tree.map(jnp.add, grad_total, grads)
    output = final_all.astype(jnp.bfloat16)
    grad_tokens = jnp.concatenate(grad_toks, axis=0)
    return (output, grad_tokens) + tuple(grad_total)


def solution(mesh):
    placed = (
        P(("twin", "dp", "fsdp"), None, None),
        P("fsdp", None),
        P("fsdp"),
        P("fsdp", None),
        P("fsdp", None),
        P("fsdp"),
        P("fsdp", None),
        P("fsdp"),
        P("fsdp"),
        P("fsdp"),
        P("fsdp", None),
        P("fsdp"),
        P("fsdp", None),
        P("fsdp"),
        P("fsdp"),
        P("fsdp"),
        P(("twin", "dp", "fsdp"), None),
        P(),
    )
    return jax.shard_map(
        per_device,
        mesh=mesh,
        in_specs=placed,
        out_specs=(
            P(("twin", "dp", "fsdp"), None, None),
            P(("twin", "dp", "fsdp"), None, None),
            P("fsdp", None),
            P("fsdp"),
            P("fsdp", None),
            P("fsdp", None),
            P("fsdp"),
            P("fsdp", None),
            P("fsdp"),
            P("fsdp"),
            P("fsdp"),
            P("fsdp", None),
            P("fsdp"),
            P("fsdp", None),
            P("fsdp"),
            P("fsdp"),
            P("fsdp"),
        ),
        check_vma=False,
    )
```

profile of v0, /device:TPU:0, one launch (start us, length us, event | category | flops | bytes accessed | tf_op | source)
XLA Modules:
  0.0 1291.8 jit_solution(9806897529139529662)
XLA Ops:
  14.7 21.7 %all-reduce.29 = (bf16[768]{0:T(1024)(128)(2,1)S(1)}, bf16[768]{0:T(1024)(128)(2,1)S(1)}, bf16[768]{0:T(1024)(128)(2,1)S(1)}, bf16[768]{0:T(1024)(128)(2,1)S(1)}...) all-reduce(bf16[768]{0:T(1024)(128)(2,1)S(1)} %dynamic-update-slice, ...), channel_id=1, replica_groups=mesh['twin'=2,'dp'=4,'fsdp'=4] {'fsdp'}, use_global_device_ids=true, to_apply=%add | all-reduce | flops 6144 | bytes 24576
  36.8 13.6 %all-gather = bf16[4,1,768]{2,1,0:T(2,128)(2,1)S(1)} all-gather(bf16[1,1,768]{2,1,0:T(2,128)(2,1)S(1)} %reshape.386), channel_id=1, replica_groups=mesh['twin'=2,'dp'=4,'fsdp'=4] {'fsdp'}, dimensions={0}, use_global_device_ids=true | all-gather | bytes 7680 | tf_op jit(solution)/shard_map/all_gather | solution.py:385
  56.7 17.5 %all-gather.8.cloned.1.call-done = bf16[768,768]{1,0:T(8,128)(2,1)} async-done(((bf16[192,768]{1,0:T(8,128)(2,1)}), bf16[768,768]{1,0:T(8,128)(2,1)}) %all-gather.8.cloned.1.call-update) | async-done | bytes 1179664 | tf_op jit(solution)/shard_map/all_gather | solution.py:378
  84.9 20.4 %all-gather.12.cloned.1.call-done = bf16[768,768]{1,0:T(8,128)(2,1)} async-done(((bf16[192,768]{1,0:T(8,128)(2,1)}), bf16[768,768]{1,0:T(8,128)(2,1)}) %all-gather.12.cloned.1.call-update) | async-done | bytes 1179664 | tf_op jit(solution)/shard_map/all_gather | solution.py:377
  123.8 12.5 all-gather.14.cloned.1.call-done
  152.4 73.9 %all-gather.16.cloned.1.call-done = bf16[768,3072]{1,0:T(8,128)(2,1)} async-done(((bf16[192,3072]{1,0:T(8,128)(2,1)}), bf16[768,3072]{1,0:T(8,128)(2,1)}) %all-gather.16.cloned.1.call-update) | async-done | bytes 4718608 | tf_op jit(solution)/shard_map/all_gather | solution.py:384
  233.9 7.8 multiply_convert_fusion.3
  241.7 73.9 %all-gather.18.cloned.1.call-done = bf16[3072,768]{1,0:T(8,128)(2,1)} async-done(((bf16[768,768]{1,0:T(8,128)(2,1)}), bf16[3072,768]{1,0:T(8,128)(2,1)}) %all-gather.18.cloned.1.call-update) | async-done | bytes 4718608 | tf_op jit(solution)/shard_map/all_gather | solution.py:386
  328.1 73.5 %all_gather.94 = bf16[512,768]{1,0:T(8,128)(2,1)S(1)} all-gather(bf16[16,768]{1,0:T(8,128)(2,1)S(1)} %bitcast.221), channel_id=1, replica_groups=mesh['twin'=2,'dp'=4,'fsdp'=4] {'twin','dp','fsdp'}, dimensions={0}, use_global_device_ids=true | all-gather | bytes 811008 | tf_op jit(solution)/shard_map/all_gather | solution.py:400
  407.8 100.1 %reduce-scatter.26.cloned.1.call-done = f32[16,768]{1,0:T(8,128)} async-done(((f32[512,768]{1,0:T(8,128)}), f32[16,768]{1,0:T(8,128)}) %reduce-scatter.26.cloned.1.call-update) | async-done | bytes 49168 | tf_op jit(solution)/shard_map/reduce_scatter | solution.py:439
  514.3 9.6 fusion.133
  542.4 8.7 bitcast_reduce_fusion
  562.5 8.2 bitcast_reduce_fusion.2
  576.0 9.5 multiply_reduce_fusion
  611.0 9.5 multiply_reduce_fusion.1
  688.3 20.1 %all-reduce.28 = (bf16[768]{0:T(1024)(128)(2,1)S(1)}, bf16[768]{0:T(1024)(128)(2,1)S(1)}, bf16[768]{0:T(1024)(128)(2,1)S(1)}, bf16[768]{0:T(1024)(128)(2,1)S(1)}...) all-reduce(bf16[768]{0:T(1024)(128)(2,1)S(1)} %reduce_sum.467, ...), channel_id=6, replica_groups=mesh['twin'=2,'dp'=4,'fsdp'=4] {'fsdp'}, use_global_device_ids=true, to_apply=%region_39.40.clone | all-reduce | flops 18432 | bytes 73728
  709.8 26.8 %all-reduce.26 = (bf16[192]{0:T(256)(128)(2,1)S(1)}, bf16[192]{0:T(256)(128)(2,1)S(1)}, bf16[192]{0:T(256)(128)(2,1)S(1)}, bf16[192]{0:T(256)(128)(2,1)S(1)}, bf...) all-reduce(bf16[192]{0:T(256)(128)(2,1)S(1)} %dynamic-slice.13, ...), channel_id=1, replica_groups=mesh['twin'=2,'dp'=4,'fsdp'=4] {'twin','dp'}, use_global_device_ids=true, to_apply=%region_40.41 | all-reduce | flops 4608 | bytes 18432 | tf_op jit(solution)/shard_map/psum | solution.py:326
  753.5 13.9 %reduce-scatter.28.cloned.1.call-done = bf16[192,768]{1,0:T(8,128)(2,1)} async-done(((bf16[768,768]{1,0:T(8,128)(2,1)}), bf16[192,768]{1,0:T(8,128)(2,1)}) %reduce-scatter.28.cloned.1.call-update) | async-done | bytes 294928 | tf_op jit(solution)/shard_map/reduce_scatter | solution.py:293
  767.4 30.1 %reduce-scatter.30.cloned.1.call-done = bf16[192,768]{1,0:T(8,128)(2,1)} async-done(((bf16[768,768]{1,0:T(8,128)(2,1)}), bf16[192,768]{1,0:T(8,128)(2,1)}) %reduce-scatter.30.cloned.1.call-update) | async-done | bytes 294928 | tf_op jit(solution)/shard_map/reduce_scatter | solution.py:293
  797.5 86.1 %reduce-scatter.38.cloned.1.call-done = bf16[768,768]{1,0:T(8,128)(2,1)} async-done(((bf16[3072,768]{1,0:T(8,128)(2,1)}), bf16[768,768]{1,0:T(8,128)(2,1)}) %reduce-scatter.38.cloned.1.call-update) | async-done | bytes 1179664 | tf_op jit(solution)/shard_map/reduce_scatter | solution.py:311
  883.6 88.0 %reduce-scatter.36.cloned.1.call-done = bf16[768,768]{1,0:T(8,128)(2,1)} async-done(((bf16[3072,768]{1,0:T(8,128)(2,1)}), bf16[768,768]{1,0:T(8,128)(2,1)}) %reduce-scatter.36.cloned.1.call-update) | async-done | bytes 1179664 | tf_op jit(solution)/shard_map/reduce_scatter | solution.py:311
  971.6 88.0 %reduce-scatter.32.cloned.1.call-done = bf16[192,3072]{1,0:T(8,128)(2,1)} async-done(((bf16[768,3072]{1,0:T(8,128)(2,1)}), bf16[192,3072]{1,0:T(8,128)(2,1)}) %reduce-scatter.32.cloned.1.call-update) | async-done | bytes 1179664 | tf_op jit(solution)/shard_map/reduce_scatter | solution.py:305
  1059.6 88.1 %reduce-scatter.34.cloned.1.call-done = bf16[192,3072]{1,0:T(8,128)(2,1)} async-done(((bf16[768,3072]{1,0:T(8,128)(2,1)}), bf16[192,3072]{1,0:T(8,128)(2,1)}) %reduce-scatter.34.cloned.1.call-update) | async-done | bytes 1179664 | tf_op jit(solution)/shard_map/reduce_scatter | solution.py:305
  1160.7 113.4 %all-reduce.32.cloned.1.call-done = (bf16[192,768]{0,1:T(8,128)(2,1)}, bf16[192,768]{0,1:T(8,128)(2,1)}, bf16[192,768]{0,1:T(8,128)(2,1)}, bf16[192,768]{0,1:T(8...) async-done(((bf16[192,768]{0,1:T(8,128)(2,1)}, ...) | async-done | bytes 7077904 | tf_op jit(solution)/shard_map/psum | solution.py:325
  (471 shorter events, 258.8 us)
Async XLA Ops:
  7.2 44.4 %all-gather.10.cloned.1.call-start = ((), (), s32[]{:S(2)}) async-start(), calls=%async_computation.14 | async-start | bytes 1474560 | tf_op jit(solution)/shard_map/all_gather | solution.py:375
  7.9 66.3 %all-gather.8.cloned.1.call-start = ((), (), s32[]{:S(2)}) async-start(), calls=%async_computation.13 | async-start | bytes 1474560 | tf_op jit(solution)/shard_map/all_gather | solution.py:378
  8.8 96.5 %all-gather.12.cloned.1.call-start = ((), (), s32[]{:S(2)}) async-start(), calls=%async_computation.15 | async-start | bytes 1474560 | tf_op jit(solution)/shard_map/all_gather | solution.py:377
  9.5 126.7 %all-gather.14.cloned.1.call-start = ((), (), s32[]{:S(2)}) async-start(), calls=%async_computation.16 | async-start | bytes 1474560 | tf_op jit(solution)/shard_map/all_gather | solution.py:380
  10.1 216.2 %all-gather.16.cloned.1.call-start = ((), (), s32[]{:S(2)}) async-start(), calls=%async_computation.17 | async-start | bytes 5898240 | tf_op jit(solution)/shard_map/all_gather | solution.py:384
  10.7 304.9 %all-gather.18.cloned.1.call-start = ((), (), s32[]{:S(2)}) async-start(), calls=%async_computation.18 | async-start | bytes 5898240 | tf_op jit(solution)/shard_map/all_gather | solution.py:386
  11.3 496.7 %reduce-scatter.26.cloned.1.call-start = ((), (), s32[]{:S(2)}) async-start(), calls=%async_computation.19 | async-start | bytes 1622016 | tf_op jit(solution)/shard_map/reduce_scatter | solution.py:439
  11.4 314.5 %copy-start.57 = (f32[2,8]{1,0:T(2,128)}, f32[2,8]{1,0:T(2,128)S(1)}, u32[]{:S(2)}) copy-start(f32[2,8]{1,0:T(2,128)S(1)} %slice_convert_fusion) | copy-start | bytes 196
  36.5 285.3 %copy-start.53 = (f32[768]{0:T(1024)}, f32[768]{0:T(1024)S(1)}, u32[]{:S(2)}) copy-start(f32[768]{0:T(1024)S(1)} %convert_element_type.474) | copy-start | bytes 9220
  36.5 285.3 %copy-start.70 = (f32[768]{0:T(1024)}, f32[768]{0:T(1024)S(1)}, u32[]{:S(2)}) copy-start(f32[768]{0:T(1024)S(1)} %convert_element_type.475) | copy-start | bytes 9220
  50.4 180.8 %copy-start.55 = (f32[4,1,768]{2,1,0:T(1,128)}, f32[4,1,768]{2,1,0:T(1,128)S(1)}, u32[]{:S(2)}) copy-start(f32[4,1,768]{2,1,0:T(1,128)S(1)} %convert_element_type.581) | copy-start | bytes 36868
  407.0 335.2 %reduce-scatter.50.cloned.1.call-start = ((), (), s32[]{:S(2)}) async-start(), calls=%async_computation.31 | async-start | bytes 1474560
  556.3 187.8 %reduce-scatter.48.cloned.1.call-start = ((), (), s32[]{:S(2)}) async-start(), calls=%async_computation.30 | async-start | bytes 1474560
  575.7 170.2 %reduce-scatter.42.cloned.1.call-start = ((), (), s32[]{:S(2)}) async-start(), calls=%async_computation.27 | async-start | bytes 1474560
  600.4 147.5 %reduce-scatter.46.cloned.1.call-start = ((), (), s32[]{:S(2)}) async-start(), calls=%async_computation.29 | async-start | bytes 1474560
  610.7 139.0 %reduce-scatter.40.cloned.1.call-start = ((), (), s32[]{:S(2)}) async-start(), calls=%async_computation.26 | async-start | bytes 1474560
  635.6 116.0 %reduce-scatter.44.cloned.1.call-start = ((), (), s32[]{:S(2)}) async-start(), calls=%async_computation.28 | async-start | bytes 1474560
  645.9 121.5 %reduce-scatter.28.cloned.1.call-start = ((), (), s32[]{:S(2)}) async-start(), calls=%async_computation.20 | async-start | bytes 1474560 | tf_op jit(solution)/shard_map/reduce_scatter | solution.py:293
  648.9 148.6 %reduce-scatter.30.cloned.1.call-start = ((), (), s32[]{:S(2)}) async-start(), calls=%async_computation.21 | async-start | bytes 1474560 | tf_op jit(solution)/shard_map/reduce_scatter | solution.py:293
  651.9 231.7 %reduce-scatter.38.cloned.1.call-start = ((), (), s32[]{:S(2)}) async-start(), calls=%async_computation.25 | async-start | bytes 5898240 | tf_op jit(solution)/shard_map/reduce_scatter | solution.py:311
  659.6 312.0 %reduce-scatter.36.cloned.1.call-start = ((), (), s32[]{:S(2)}) async-start(), calls=%async_computation.24 | async-start | bytes 5898240 | tf_op jit(solution)/shard_map/reduce_scatter | solution.py:311
  666.9 392.7 %reduce-scatter.32.cloned.1.call-start = ((), (), s32[]{:S(2)}) async-start(), calls=%async_computation.22 | async-start | bytes 5898240 | tf_op jit(solution)/shard_map/reduce_scatter | solution.py:305
  675.0 472.7 %reduce-scatter.34.cloned.1.call-start = ((), (), s32[]{:S(2)}) async-start(), calls=%async_computation.23 | async-start | bytes 5898240 | tf_op jit(solution)/shard_map/reduce_scatter | solution.py:305
  683.1 591.0 %all-reduce.32.cloned.1.call-start = ((), (), s32[]{:S(2)}) async-start(), calls=%async_computation.32 | async-start | bytes 15335424 | tf_op jit(solution)/shard_map/psum | solution.py:325
  (113 other events, 1324.5 us)
Sparse Core Ops, SparseCore 0:
  9.6 33.4 all-gather.9
  44.6 29.5 all-gather.7
  75.8 29.4 all-gather.11
  106.7 29.4 all-gather.13
  137.7 88.6 all-gather.15
  227.7 87.7 all-gather.17
  407.1 100.8 reduce-scatter.25
  556.4 28.3 reduce-scatter.49
  587.1 27.9 reduce-scatter.47
  617.2 27.9 reduce-scatter.41
  647.5 27.9 reduce-scatter.45
  677.6 29.3 reduce-scatter.39
  709.3 27.9 reduce-scatter.43
  739.5 27.9 reduce-scatter.27
  769.6 27.9 reduce-scatter.29
  799.7 83.8 reduce-scatter.37
  885.8 85.7 reduce-scatter.35
  973.8 85.7 reduce-scatter.31
  1061.9 85.7 reduce-scatter.33
  1153.6 120.4 all-reduce.31
where the time goes:
time: 1300 us; the launch traced here: 1290 us
  waiting for transfers between devices  810 us (62%)
  matrix products  192 us (15%)
  blocking collectives  156 us (12%)
  local copies, waits for them, and re-layouts  67.7 us (5%)
  other arithmetic  46.8 us (4%)
  between operations  18 us (1%)
    reduce_scatter x2, waiting for transfers between devices, reduce_grads(): lax.psum_scatter(grad_w_inner.astype(jnp.bfloat16), 'fsdp', scatter_dimen...  176 us
    reduce_scatter x2, waiting for transfers between devices, reduce_grads(): lax.psum_scatter(grad_w_outer.astype(jnp.bfloat16), 'fsdp', scatter_dimen...  174 us
    psum x1, waiting for transfers between devices, reduce_grads(): lax.psum(shard_w_query.astype(jnp.bfloat16), ('twin', 'dp'))  113 us
    reduce_scatter x1, waiting for transfers between devices, per_device(): lax.psum_scatter(term, ('twin', 'dp', 'fsdp'), scatter_dimension=0, tiled...  100 us
    all_gather x1, waiting for transfers between devices, per_device(): lax.all_gather(w_inner, 'fsdp', axis=0, tiled=True)  73.9 us
    all_gather x1, waiting for transfers between devices, per_device(): lax.all_gather(w_outer, 'fsdp', axis=0, tiled=True)  73.9 us
    all_gather x1, blocking collectives, per_device(): lax.all_gather(pooled_low, ('twin', 'dp', 'fsdp'), axis=0, tiled=True)  73.5 us
    unnamed x285, local copies, waits for them, and re-layouts  54.2 us
  transfers between devices with their start and end apart: 20, of which 13 were waited for; matrix products, arithmetic and copies ran while one was open for 16% of the time, Pallas kernels for 0%

commit v1 on v0

v1 whole, which is shorter than its diff:
```python
import functools

import jax
import jax.numpy as jnp
from jax import lax
from jax.sharding import PartitionSpec as P

H = 12
HD = 64
SEG = 8


norm_eps = 1e-12
pool_eps = 1e-06
sim_scale = 20.0


def cross_dot(left, right):
    return lax.dot_general(
        left, right, (((0,), (0,)), ((), ())), preferred_element_type=jnp.float32
    )


def back_dot(left, right):
    return lax.dot_general(
        left, right, (((1,), (1,)), ((), ())), preferred_element_type=jnp.float32
    )


def plain_dot(left, right):
    return jnp.dot(left, right, preferred_element_type=jnp.float32)


def segment_ids(lengths, seq_len):
    ends = jnp.cumsum(lengths, axis=1, dtype=jnp.int32)
    position = jnp.arange(seq_len, dtype=jnp.int32)
    return jnp.sum((position[None, :, None] >= ends[:, None, :]).astype(jnp.int32), axis=2)


def normalize(hidden):
    centred = hidden - jnp.mean(hidden, axis=-1, keepdims=True)
    inv_dev = lax.rsqrt(jnp.mean(centred * centred, axis=-1, keepdims=True) + norm_eps)
    return (centred * inv_dev, inv_dev)


def norm_back(grad_normed, normed, inv_dev):
    return inv_dev * (
        grad_normed
        - jnp.mean(grad_normed, axis=-1, keepdims=True)
        - normed * jnp.mean(grad_normed * normed, axis=-1, keepdims=True)
    )


def gelu_parts(inner):
    cdf_value = 0.5 * (1.0 + lax.erf(inner * 0.7071067811865476))
    slope = cdf_value + inner * jnp.exp(-0.5 * inner * inner) * 0.3989422804014327
    return (cdf_value, slope)


def masked_scores(query, keys, seg_row):
    scores = jnp.einsum("qhd,khd->hqk", query, keys, preferred_element_type=jnp.float32) * HD ** (
        -0.5
    )
    same = seg_row[:, None] == seg_row[None, :]
    return jnp.where(same[None], scores, -1e30)


def attend(item):
    query, keys, values, seg_row = item
    scores = masked_scores(query, keys, seg_row)
    row_max = jnp.max(scores, axis=2, keepdims=True)
    exp_scores = jnp.exp(scores - row_max)
    row_sum = jnp.sum(exp_scores, axis=2, keepdims=True)
    attn_prob = (exp_scores / row_sum).astype(jnp.bfloat16)
    context = jnp.einsum("hqk,khd->qhd", attn_prob, values, preferred_element_type=jnp.float32)
    return (context.astype(jnp.bfloat16), row_max[:, :, 0] + jnp.log(row_sum[:, :, 0]))


def attend_back(item):
    query, keys, values, seg_row, log_total, grad_ctx = item
    attn_prob = jnp.exp(masked_scores(query, keys, seg_row) - log_total[:, :, None])
    grad_values = jnp.einsum(
        "hqk,qhd->khd", attn_prob.astype(jnp.bfloat16), grad_ctx, preferred_element_type=jnp.float32
    )
    grad_prob = jnp.einsum("qhd,khd->hqk", grad_ctx, values, preferred_element_type=jnp.float32)
    grad_scores = attn_prob * (grad_prob - jnp.sum(attn_prob * grad_prob, axis=2, keepdims=True))
    grad_scores = grad_scores.astype(jnp.bfloat16)
    grad_query = jnp.einsum(
        "hqk,khd->qhd", grad_scores, keys, preferred_element_type=jnp.float32
    ) * HD ** (-0.5)
    grad_keys = jnp.einsum(
        "hqk,qhd->khd", grad_scores, query, preferred_element_type=jnp.float32
    ) * HD ** (-0.5)
    return (
        grad_query.astype(jnp.bfloat16),
        grad_keys.astype(jnp.bfloat16),
        grad_values.astype(jnp.bfloat16),
    )


def xor_pairs(count, bit):
    return [(i, i ^ bit) for i in range(count)]


def place(parts, spots, axis):
    shape = list(parts[0].shape)
    shape.insert(axis, len(parts))
    out = jnp.zeros(shape, parts[0].dtype)
    for part, spot in zip(parts, spots):
        out = lax.dynamic_update_index_in_dim(out, part, spot, axis)
    return out


def swap(value, axis_name, count, bit):
    return lax.ppermute(value, axis_name, xor_pairs(count, bit))


def join(value, axis_name, count, bit, axis):
    other = swap(value, axis_name, count, bit)
    own_bit = (lax.axis_index(axis_name) // bit) % 2
    return place([value, other], [own_bit, 1 - own_bit], axis)


def gather_depth(value, depth):
    if depth != 4:
        return lax.all_gather(value, "fsdp", axis=0)
    z = lax.axis_index("fsdp")
    parts = [value] + [swap(value, "fsdp", depth, s) for s in range(1, depth)]
    return place(parts, [z ^ s for s in range(depth)], 0)


def sum_depth(value, depth):
    if depth != 4:
        return lax.psum_scatter(value, "fsdp", scatter_dimension=0).astype(jnp.float32)
    z = lax.axis_index("fsdp")
    pick = lambda s: lax.dynamic_index_in_dim(value, z ^ s, 0, keepdims=False)
    total = pick(0).astype(jnp.float32)
    for s in range(1, depth):
        total = total + swap(pick(s), "fsdp", depth, s).astype(jnp.float32)
    return total


def halve(value, axis_name, count, bit, axis):
    own_bit = (lax.axis_index(axis_name) // bit) % 2
    mine = lax.dynamic_index_in_dim(value, own_bit, axis, keepdims=False)
    sent = lax.dynamic_index_in_dim(value, 1 - own_bit, axis, keepdims=False).astype(jnp.bfloat16)
    got = swap(sent, axis_name, count, bit)
    return (mine.astype(jnp.float32) + got.astype(jnp.float32)).astype(jnp.bfloat16)


def both(value, axis_name, count, bit):
    low = value.astype(jnp.bfloat16)
    got = swap(low, axis_name, count, bit)
    return (low.astype(jnp.float32) + got.astype(jnp.float32)).astype(jnp.bfloat16)


def forward_rows(tok, seg_all, weights):
    (
        w_query,
        b_query,
        w_key,
        w_value,
        b_value,
        w_out,
        b_out,
        gain_attn,
        shift_attn,
        w_inner,
        b_inner,
        w_outer,
        b_outer,
        gain_ffn,
        shift_ffn,
    ) = weights
    row_count, seq_len, model_dim = tok.shape
    tok_flat = tok.reshape(row_count * seq_len, model_dim)
    head_shape = (row_count, seq_len, H, HD)
    query = (plain_dot(tok_flat, w_query) + b_query).astype(jnp.bfloat16).reshape(head_shape)
    keys = plain_dot(tok_flat, w_key).astype(jnp.bfloat16).reshape(head_shape)
    values = (plain_dot(tok_flat, w_value) + b_value).astype(jnp.bfloat16).reshape(head_shape)
    context, log_total = lax.map(attend, (query, keys, values, seg_all))
    context = context.reshape(row_count * seq_len, model_dim)
    normed_attn, inv_attn = normalize(
        tok_flat.astype(jnp.float32) + plain_dot(context, w_out) + b_out
    )
    mid_state = normed_attn * gain_attn + shift_attn
    mid_low = mid_state.astype(jnp.bfloat16)
    inner = plain_dot(mid_low, w_inner) + b_inner
    cdf_value, slope = gelu_parts(inner)
    activ = (inner * cdf_value).astype(jnp.bfloat16)
    normed_ffn, inv_ffn = normalize(mid_state + plain_dot(activ, w_outer) + b_outer)
    final = normed_ffn * gain_ffn + shift_ffn
    saved = (
        query,
        keys,
        values,
        log_total,
        context,
        normed_attn,
        inv_attn,
        mid_low,
        inner,
        activ,
        normed_ffn,
        inv_ffn,
    )
    return (final, saved)


def loss_grad(pooled_low, labels, twins, groups, depth):
    own_count, model_dim = pooled_low.shape
    half_count = labels.shape[0]
    same = pooled_low
    if groups == 4:
        same = join(same, "dp", groups, 1, 0)
        same = join(same, "dp", groups, 2, 0)
        same = gather_depth(same, depth)
        same = same.reshape(depth, groups, own_count, model_dim).swapaxes(0, 1)
        same = same.reshape(half_count, model_dim)
    else:
        same = lax.all_gather(same, ("dp", "fsdp"), axis=0, tiled=True)
    other = swap(same, "twin", twins, 1)
    twin_side = lax.axis_index("twin")
    first = lax.axis_index(("dp", "fsdp")) * own_count
    own_f = pooled_low.astype(jnp.float32)
    same_f = same.astype(jnp.float32)
    other_f = other.astype(jnp.float32)
    inv_own = lax.rsqrt(jnp.sum(own_f * own_f, axis=1) + pool_eps)
    inv_same = lax.rsqrt(jnp.sum(same_f * same_f, axis=1) + pool_eps)
    inv_other = lax.rsqrt(jnp.sum(other_f * other_f, axis=1) + pool_eps)
    similar = sim_scale * back_dot(same, other) * inv_same[:, None] * inv_other[None, :]
    col_max = jnp.max(similar, axis=0, keepdims=True)
    col_log = col_max[0] + jnp.log(jnp.sum(jnp.exp(similar - col_max), axis=0))
    own_sim = lax.dynamic_slice_in_dim(similar, first, own_count, 0)
    row_max = jnp.max(own_sim, axis=1, keepdims=True)
    row_log = row_max[:, 0] + jnp.log(jnp.sum(jnp.exp(own_sim - row_max), axis=1))
    col_index = jnp.arange(half_count, dtype=jnp.int32)
    own_labels = lax.dynamic_slice_in_dim(labels, first, own_count, 0)
    own_index = first + jnp.arange(own_count, dtype=jnp.int32)
    target = jnp.where(
        twin_side == 0,
        col_index[None, :] == own_labels[:, None],
        labels[None, :] == own_index[:, None],
    ).astype(jnp.float32)
    grad_sim = (
        jnp.exp(own_sim - row_log[:, None]) + jnp.exp(own_sim - col_log[None, :]) - 2.0 * target
    )
    grad_raw = sim_scale * grad_sim * inv_own[:, None] * inv_other[None, :]
    return (
        jnp.dot(grad_raw, other_f, precision=lax.Precision.HIGHEST)
        - (jnp.sum(grad_sim * own_sim, axis=1) * inv_own * inv_own)[:, None] * own_f
    )


def per_device(
    sizes,
    tokens,
    w_query,
    b_query,
    w_key,
    w_value,
    b_value,
    w_out,
    b_out,
    gain_attn,
    shift_attn,
    w_inner,
    b_inner,
    w_outer,
    b_outer,
    gain_ffn,
    shift_ffn,
    lengths,
    labels,
):
    twins, groups, depth = sizes
    row_total, seq_len, model_dim = tokens.shape
    token_count = row_total * seq_len
    shard = w_query.shape[0]
    half = shard // 2
    inner_dim = w_inner.shape[1]
    twin = lax.axis_index("twin")
    group = lax.axis_index("dp")
    eighth = twin * 4 + group

    square = jnp.stack([w_query, w_key, w_value, w_out]).reshape(8, half, model_dim)
    piece_a = lax.dynamic_index_in_dim(square, eighth, 0, keepdims=False)
    piece_b = lax.dynamic_slice(
        w_inner, ((eighth % 2) * half, (eighth // 2) * model_dim), (half, model_dim)
    )
    piece_c = lax.dynamic_slice_in_dim(w_outer, eighth * half, half, 0)
    vectors = jnp.concatenate(
        [b_query, b_value, b_out, gain_attn, shift_attn, b_outer, gain_ffn, shift_ffn, b_inner]
    )
    vec_size = vectors.shape[0]
    vec_rows = -(-vec_size // model_dim)
    vec_block = jnp.pad(vectors, (0, vec_rows * model_dim - vec_size)).reshape(vec_rows, model_dim)
    deep_a = gather_depth(jnp.concatenate([piece_a, vec_block]), depth)
    vec_all = deep_a[:, half:].reshape(depth, vec_rows * model_dim)
    full = deep_a[:, :half]
    full = join(full, "dp", groups, 1, 1)
    full = join(full, "dp", groups, 2, 0)
    full = join(full, "twin", twins, 1, 0)
    full = full.reshape(4, model_dim, model_dim)
    wide = gather_depth(piece_b, depth)
    wide = join(wide, "dp", groups, 2, 2)
    wide = wide.reshape(depth, half, 2 * model_dim)
    wide = join(wide, "dp", groups, 1, 1)
    wide = wide.reshape(model_dim, 2 * model_dim)
    wide = join(wide, "twin", twins, 1, 1).reshape(model_dim, inner_dim)
    tall = gather_depth(piece_c, depth)
    tall = join(tall, "dp", groups, 1, 1)
    tall = join(tall, "dp", groups, 2, 1)
    tall = join(tall, "twin", twins, 1, 1).reshape(inner_dim, model_dim)
    small = vec_all[:, : 8 * shard].reshape(depth, 8, shard).swapaxes(0, 1).reshape(8, model_dim)
    full_b_inner = vec_all[:, 8 * shard : vec_size].reshape(inner_dim)
    weights = (
        full[0], small[0], full[1], full[2], small[1], full[3], small[2], small[3], small[4],
        wide, full_b_inner, tall, small[5], small[6], small[7],
    )

    seg_all = segment_ids(lengths, seq_len)
    member = (seg_all[:, None, :] == jnp.arange(SEG, dtype=jnp.int32)[None, :, None]).astype(
        jnp.float32
    )
    counts = lengths[:, :SEG].astype(jnp.float32)
    final, saved = forward_rows(tokens, seg_all, weights)
    output = final.astype(jnp.bfloat16).reshape(row_total, seq_len, model_dim)
    pooled_f = (
        jnp.einsum(
            "rst,rtd->rsd",
            member,
            final.reshape(row_total, seq_len, model_dim),
            precision=lax.Precision.HIGHEST,
        )
        / counts[:, :, None]
    )
    pooled_low = pooled_f.reshape(row_total * SEG, model_dim).astype(jnp.bfloat16)
    grad_pooled = loss_grad(pooled_low, labels, twins, groups, depth)
    grad_scaled = grad_pooled.reshape(row_total, SEG, model_dim) / counts[:, :, None]
    grad_final = jnp.einsum(
        "rst,rsd->rtd", member, grad_scaled, precision=lax.Precision.HIGHEST
    ).reshape(token_count, model_dim)

    (
        query,
        keys,
        values,
        log_total,
        context,
        normed_attn,
        inv_attn,
        mid_low,
        inner,
        activ,
        normed_ffn,
        inv_ffn,
    ) = saved
    tok_flat = tokens.reshape(token_count, model_dim)
    f_w_query, _, f_w_key, f_w_value, _, f_w_out, _, f_gain_attn, _, _, _, _, _, f_gain_ffn, _ = weights
    grad_gain_ffn = jnp.sum(grad_final * normed_ffn, axis=0)
    grad_shift_ffn = jnp.sum(grad_final, axis=0)
    grad_h2 = norm_back(grad_final * f_gain_ffn, normed_ffn, inv_ffn)
    grad_branch = grad_h2.astype(jnp.bfloat16)
    grad_tall = cross_dot(activ, grad_branch).reshape(depth, 2, 2, 2, half, model_dim)
    grad_tall = halve(grad_tall, "twin", twins, 1, 1)
    grad_tall = halve(grad_tall, "dp", groups, 1, 2)
    grad_tall = halve(grad_tall, "dp", groups, 2, 1)
    done_c = sum_depth(grad_tall, depth)
    grad_b_outer = jnp.sum(grad_branch, axis=0, dtype=jnp.float32)
    _, slope = gelu_parts(inner)
    grad_inner = (back_dot(grad_branch, tall) * slope).astype(jnp.bfloat16)
    grad_wide = cross_dot(mid_low, grad_inner).reshape(depth, 2, half, 2, 2 * model_dim)
    grad_wide = halve(grad_wide, "twin", twins, 1, 3).reshape(depth, 2, half, 2, model_dim)
    grad_wide = halve(grad_wide, "dp", groups, 2, 3)
    grad_wide = halve(grad_wide, "dp", groups, 1, 1)
    done_b = sum_depth(grad_wide, depth)
    grad_b_inner = jnp.sum(grad_inner, axis=0, dtype=jnp.float32)
    grad_mid = grad_h2 + back_dot(grad_inner, wide)
    grad_gain_attn = jnp.sum(grad_mid * normed_attn, axis=0)
    grad_shift_attn = jnp.sum(grad_mid, axis=0)
    grad_h1 = norm_back(grad_mid * f_gain_attn, normed_attn, inv_attn)
    grad_attn = grad_h1.astype(jnp.bfloat16)
    grad_w_out = cross_dot(context, grad_attn)
    grad_b_out = jnp.sum(grad_attn, axis=0, dtype=jnp.float32)
    grad_ctx = back_dot(grad_attn, f_w_out).astype(jnp.bfloat16).reshape(row_total, seq_len, H, HD)
    grad_query, grad_keys, grad_values = lax.map(
        attend_back, (query, keys, values, seg_all, log_total, grad_ctx)
    )
    flat_shape = (token_count, model_dim)
    grad_query = grad_query.reshape(flat_shape)
    grad_keys = grad_keys.reshape(flat_shape)
    grad_values = grad_values.reshape(flat_shape)
    grad_w_query = cross_dot(tok_flat, grad_query)
    grad_b_query = jnp.sum(grad_query, axis=0, dtype=jnp.float32)
    grad_w_key = cross_dot(tok_flat, grad_keys)
    grad_w_value = cross_dot(tok_flat, grad_values)
    grad_b_value = jnp.sum(grad_values, axis=0, dtype=jnp.float32)
    grad_tok = (
        grad_h1
        + back_dot(grad_query, f_w_query)
        + back_dot(grad_keys, f_w_key)
        + back_dot(grad_values, f_w_value)
    )
    grad_tokens = grad_tok.astype(jnp.bfloat16).reshape(row_total, seq_len, model_dim)

    grad_square = jnp.stack([grad_w_query, grad_w_key, grad_w_value, grad_w_out]).reshape(
        2, 2, depth, 2, half, model_dim
    )
    vec_grads = jnp.stack(
        [
            grad_b_query,
            grad_b_value,
            grad_b_out,
            grad_gain_attn,
            grad_shift_attn,
            grad_b_outer,
            grad_gain_ffn,
            grad_shift_ffn,
        ]
    )
    vec_grads = vec_grads.reshape(8, depth, shard).swapaxes(0, 1).reshape(depth, 8 * shard)
    vec_grads = jnp.concatenate([vec_grads, grad_b_inner.reshape(depth, 4 * shard)], axis=1)
    vec_grads = jnp.pad(vec_grads, ((0, 0), (0, vec_rows * model_dim - vec_size)))
    vec_grads = both(vec_grads, "twin", twins, 1)
    vec_grads = both(vec_grads, "dp", groups, 1)
    vec_grads = both(vec_grads, "dp", groups, 2)
    grad_square = halve(grad_square, "twin", twins, 1, 0)
    grad_square = halve(grad_square, "dp", groups, 1, 2)
    grad_square = halve(grad_square, "dp", groups, 2, 0)
    last = jnp.concatenate([grad_square, vec_grads.reshape(depth, vec_rows, model_dim)], axis=1)
    last = sum_depth(last, depth)
    vec_done = last[half:].reshape(vec_rows * model_dim)
    pieces = jnp.stack([last[:half], done_b, done_c]).astype(jnp.bfloat16)
    pieces = join(pieces, "dp", groups, 1, 1)
    pieces = join(pieces, "dp", groups, 2, 1)
    pieces = join(pieces, "twin", twins, 1, 1)
    pieces = pieces.astype(jnp.float32)
    out_square = pieces[0].reshape(4, shard, model_dim)
    out_wide = pieces[1].reshape(4, shard, model_dim).swapaxes(0, 1).reshape(shard, inner_dim)
    out_tall = pieces[2].reshape(4 * shard, model_dim)
    vec = vec_done[: 8 * shard].reshape(8, shard)
    return (
        output,
        grad_tokens,
        out_square[0],
        vec[0],
        out_square[1],
        out_square[2],
        vec[1],
        out_square[3],
        vec[2],
        vec[3],
        vec[4],
        out_wide,
        vec_done[8 * shard : vec_size],
        out_tall,
        vec[5],
        vec[6],
        vec[7],
    )


def solution(mesh):
    placed = (
        P(("twin", "dp", "fsdp"), None, None),
        P("fsdp", None),
        P("fsdp"),
        P("fsdp", None),
        P("fsdp", None),
        P("fsdp"),
        P("fsdp", None),
        P("fsdp"),
        P("fsdp"),
        P("fsdp"),
        P("fsdp", None),
        P("fsdp"),
        P("fsdp", None),
        P("fsdp"),
        P("fsdp"),
        P("fsdp"),
        P(("twin", "dp", "fsdp"), None),
        P(),
    )
    sizes = (mesh.shape["twin"], mesh.shape["dp"], mesh.shape["fsdp"])
    return jax.shard_map(
        functools.partial(per_device, sizes),
        mesh=mesh,
        in_specs=placed,
        out_specs=(
            P(("twin", "dp", "fsdp"), None, None),
            P(("twin", "dp", "fsdp"), None, None),
            P("fsdp", None),
            P("fsdp"),
            P("fsdp", None),
            P("fsdp", None),
            P("fsdp"),
            P("fsdp", None),
            P("fsdp"),
            P("fsdp"),
            P("fsdp"),
            P("fsdp", None),
            P("fsdp"),
            P("fsdp", None),
            P("fsdp"),
            P("fsdp"),
            P("fsdp"),
        ),
        check_vma=False,
    )
```

time: 1300 us -> 609 us (0.47)
  waiting for transfers between devices: 810 us -> 148 us
  blocking collectives: 156 us -> 0 us
  local copies, waits for them, and re-layouts: 67.7 us -> 204 us
  matrix products: 192 us -> 133 us
  starting transfers between devices: 1.6 us -> 53.8 us
  between operations: 18 us -> 2.81 us
    reduce_scatter x7 -> x0, waiting for transfers between devices: 494 us -> none  [the longest x2 176 us: reduce_grads(): lax.psum_scatter(grad_w_inner.astype(jnp.bfloat16), 'fsdp', scatter_dimen...]
    all_gather x6 -> x0, waiting for transfers between devices: 198 us -> none  [the longest x1 73.9 us: per_device(): lax.all_gather(w_inner, 'fsdp', axis=0, tiled=True)]
    ppermute x0 -> x48, waiting for transfers between devices: none -> 148 us  [swap(): return lax.ppermute(value, axis_name, xor_pairs(count, bit))]
    psum x1 -> x0, waiting for transfers between devices: 113 us -> none  [reduce_grads(): lax.psum(shard_w_query.astype(jnp.bfloat16), ('twin', 'dp'))]
    all_gather x2 -> x0, blocking collectives: 87.1 us -> none  [the longest x1 73.5 us: per_device(): lax.all_gather(pooled_low, ('twin', 'dp', 'fsdp'), axis=0, tiled=True)]
    dynamic_update_slice x0 -> x41, local copies, waits for them, and re-layouts: none -> 64.3 us  [place(): out = lax.dynamic_update_index_in_dim(out, part, spot, axis)]
    ppermute x0 -> x48, starting transfers between devices: none -> 53.8 us  [swap(): return lax.ppermute(value, axis_name, xor_pairs(count, bit))]
    unnamed x2 -> x0, blocking collectives: 41.9 us -> none
  transfers between devices with their start and end apart: 20 -> 48, of which waited for: 13 -> 18; matrix products, arithmetic and copies ran while one was open for 16% -> 29% of each run, Pallas kernels for 0% -> 0%
where the time goes in v1:
time: 609 us; the launch traced here: 597 us
  local copies, waits for them, and re-layouts  204 us (33%)
  waiting for transfers between devices  148 us (24%)
  matrix products  133 us (22%)
  other arithmetic  55 us (9%)
  starting transfers between devices  53.8 us (9%)
    ppermute x48, waiting for transfers between devices, swap(): return lax.ppermute(value, axis_name, xor_pairs(count, bit))  148 us
    dynamic_update_slice x41, local copies, waits for them, and re-layouts, place(): out = lax.dynamic_update_index_in_dim(out, part, spot, axis)  64.3 us
    ppermute x48, starting transfers between devices, swap(): return lax.ppermute(value, axis_name, xor_pairs(count, bit))  53.8 us
    dot_general x7, matrix products, back_dot(): lax.dot_general(left, right, (((1,), (1,)), ((), ())), preferred_element_...  31.3 us
    dot_general x6, matrix products, plain_dot(): return jnp.dot(left, right, preferred_element_type=jnp.float32)  25.4 us
    dot_general x6, matrix products, cross_dot(): lax.dot_general(left, right, (((0,), (0,)), ((), ())), preferred_element_...  23.8 us
    unnamed x185, local copies, waits for them, and re-layouts  17.5 us
    convert_element_type x2, other arithmetic, attend_back(): grad_scores = grad_scores.astype(jnp.bfloat16)  14.2 us
  transfers between devices with their start and end apart: 48, of which 18 were waited for; matrix products, arithmetic and copies ran while one was open for 29% of the time, Pallas kernels for 0%

profile of v1, /device:TPU:0, one launch (start us, length us, event | category | flops | bytes accessed | tf_op | source)
XLA Modules:
  0.0 596.9 jit_solution(7998379869593715263)
XLA Ops:
  35.9 12.6 %collective-permute-done.7 = bf16[96,768]{1,0:T(8,128)(2,1)S(1)} collective-permute-done((bf16[96,768]{1,0:T(8,128)(2,1)S(1)}, bf16[96,768]{1,0:T(8,128)(2,1)S(1)}, u32[]{:S(2)}, u32[]{:S(2)}) %collective-permute-start.7) | collective-permute-done | bytes 147488 | tf_op jit(solution)/shard_map/ppermute | solution.py:115
  55.5 12.0 %dynamic_update_slice.179 = bf16[4,96,2,768]{3,2,1,0:T(2,128)(2,1)S(1)} dynamic-update-slice(bf16[4,96,2,768]{3,2,1,0:T(2,128)(2,1)S(1)} %broadcast_in_dim.288, bf16[4,96,1,768]{3,2,1,0:T(2,128)(2,1)S(1)} %copy.266, s32[]{:T(128)} %copy.414, s32[]{:T(128)} %copy.414, s32[]{:T(128)S(6)} %select_n.250, s32[]{:T(128)} %copy.414) | dynamic-update-slice | bytes 1179652 | tf_op jit(solution)/shard_map/jit(dynamic_update_index_in_dim)/dynamic_update_slice | solution.py:110
  78.5 19.2 %dynamic_update_slice.180 = bf16[4,96,2,768]{3,2,1,0:T(2,128)(2,1)S(1)} dynamic-update-slice(bf16[4,96,2,768]{3,2,1,0:T(2,128)(2,1)S(1)} %dynamic_update_slice.179, bf16[4,96,1,768]{3,2,1,0:T(2,128)(2,1)} %copy.267, s32[]{:T(128)} %copy.414, s32[]{:T(128)} %copy.414, s32[]{:T(128)S(6)} %select_n.251, s32[]{:T(128)} %copy.414) | dynamic-update-slice | bytes 1179652 | tf_op jit(solution)/shard_map/jit(dynamic_update_index_in_dim)/dynamic_update_slice | solution.py:110
  112.7 13.3 %collective-permute-done.10 = bf16[4,96,1536]{2,1,0:T(8,128)(2,1)S(1)} collective-permute-done((bf16[4,96,1536]{2,1,0:T(8,128)(2,1)}, bf16[4,96,1536]{2,1,0:T(8,128)(2,1)S(1)}, u32[]{:S(2)}, u32[]{:S(2)}) %collective-permute-start.10) | collective-permute-done | bytes 1179680 | tf_op jit(solution)/shard_map/ppermute | solution.py:115
  131.0 20.0 %collective-permute-done.4 = bf16[4,2,96,768]{3,2,1,0:T(8,128)(2,1)S(1)} collective-permute-done((bf16[4,2,96,768]{3,2,1,0:T(8,128)(2,1)S(1)}, bf16[4,2,96,768]{3,2,1,0:T(8,128)(2,1)S(1)}, u32[]{:S(2)}, u32[]{:S(2)}) %collective-permute-start.4) | collective-permute-done | bytes 1179680 | tf_op jit(solution)/shard_map/ppermute | solution.py:115
  207.6 20.8 %while.26 = (s32[]{:T(128)}, bf16[2,512,12,64]{1,3,2,0:T(8,128)(2,1)}, f32[2,12,512]{2,1,0:T(8,128)S(1)}, bf16[2,512,12,64]{1,3,2,0:T(8,128)(2,1)}, s32[2,512]{1...) while((s32[]{:T(128)}, ...), condition=%wide.region_5.6_spmd, body=%wide.region_2.5_spmd.sunk | while | flops 843704320 | bytes 42172508 | solution.py:181
  236.3 8.4 %multiply_convert_fusion.3 = (bf16[1024,3072]{1,0:T(8,128)(2,1)S(1)}, f32[1024,3072]{1,0:T(8,128)}) fusion(f32[3072]{0:T(1024)S(1)} %copy-done.54, bf16[768,3072]{0,1:T(8,128)(2,1)S(1)} %bitcast.501, f32[1024,768]{1,0:T(8,128)S(1)} %get-tuple-element.328, f32[768]{0:T(1024)S(1)} %copy-done.51, f32[768]{0:T(1024)S(1)} %copy-done.43, ...), kind=kOutput, calls=%fused_computation.71 | convolution fusion | flops 4854644736 | bytes 26765312 | tf_op jit(solution)/shard_map/dot_general | solution.py:31
  290.0 12.6 %fusion.148 = (bf16[3072]{0:T(1024)(128)(2,1)}, bf16[1024,3072]{1,0:T(8,128)(2,1)S(1)}) fusion(f32[1024,3072]{1,0:T(8,128)} %get-tuple-element.330, f32[3072]{0:T(1024)S(1)} %copy-done.55, bf16[3072,768]{1,0:T(8,128)(2,1)S(1)} %bitcast.510, f32[1024,768]{1,0:T(8,128)S(1)} %get-tuple-element.284), kind=kOutput, calls=%fused_computation.340 | convolution fusion | flops 4870370304 | bytes 26757120 | tf_op jit(solution)/shard_map/dot_general | solution.py:25
  318.6 8.5 %fusion.137 = f32[768,3072]{1,0:T(8,128)} fusion(bf16[1024,3072]{1,0:T(8,128)(2,1)S(1)} %get-tuple-element.340, f32[1024,768]{1,0:T(8,128)S(1)} %copy-done.3, f32[768]{0:T(1024)S(1)} %copy-done.52, f32[768]{0:T(1024)S(1)} %copy-done.43, f32[1024]{0:T(1024)S(1)} %add_rsqrt_fusion.1, f32[1024]{0:T(1024)S(1)} %broadcast_multiply_fusion.4), kind=kOutput, calls=%fused_computation.331 | convolution fusion | flops 4835770368 | bytes 18888704 | tf_op jit(solution)/shard_map/dot_general | solution.py:19
  327.1 8.1 %fusion.132 = f32[3072,768]{1,0:T(8,128)} fusion(bf16[1024,3072]{1,0:T(8,128)(2,1)S(1)} %bitcast.560, f32[1024,768]{1,0:T(8,128)S(1)} %get-tuple-element.284), kind=kOutput, calls=%fused_computation.325 | convolution fusion | flops 4832624640 | bytes 18874368 | tf_op jit(solution)/shard_map/dot_general | solution.py:19
  348.5 48.9 %while.27 = (s32[]{:T(128)}, bf16[2,512,12,64]{1,3,2,0:T(8,128)(2,1)}, bf16[2,512,12,64]{1,3,2,0:T(8,128)(2,1)}, bf16[2,512,12,64]{1,3,2,0:T(8,128)(2,1)}, bf16[...) while((s32[]{:T(128)}, ...), condition=%wide.region_24.25_spmd, body=%wide.region_22.24_spmd.sunk | while | flops 2062673920 | bytes 147524944 | solution.py:387
  350.6 6.9 %multiply_reduce_fusion.13 = (f32[12,512]{1,0:T(8,128)S(1)}, f32[12,512,512]{1,2,0:T(8,128)}) fusion(f32[12,512,512]{1,2,0:T(8,128)S(1)} %fusion.206, f32[12,512]{1,0:T(8,128)S(1)} %dynamic-slice_bitcast_fusion.14, pred[512,512]{0,1:T(8,128)(4,1)S(1)} %broadcast_compare_fusion.5, bf16[2,512,12,64]{1,3,2,0:T(8,128)(2,1)S(1)} %copy-done.5, ...), kind=kOutput, calls=%fused_computation.24.clone.1 | convolution fusion | flops 418375680 | bytes 27059200 | tf_op jit(solution)/shard_map/while/body/eval_jaxpr/qhd,khd->hqk/dot_general | solution.py:85
  357.5 7.1 %multiply_convert_fusion.5 = bf16[12,512,512]{1,2,0:T(8,128)(2,1)S(1)} fusion(f32[12,512,512]{1,2,0:T(8,128)} %get-tuple-element.453, f32[12,512,512]{1,2,0:T(8,128)S(1)} %fusion.206, f32[12,512]{1,0:T(8,128)S(1)} %get-tuple-element.454, f32[12,512]{1,0:T(8,128)S(1)} %dynamic-slice_bitcast_fusion.14, pred[512,512]{0,1:T(8,128)(4,1)S(1)} %broadcast_compare_fusion.5), kind=kLoop, calls=%fused_computation.23.clone.1 | loop fusion | flops 18874368 | bytes 31768576 | tf_op jit(solution)/shard_map/while/body/eval_jaxpr/convert_element_type | solution.py:87
  381.9 7.1 %multiply_convert_fusion.5 = bf16[12,512,512]{1,2,0:T(8,128)(2,1)S(1)} fusion(f32[12,512,512]{1,2,0:T(8,128)} %get-tuple-element.453, f32[12,512,512]{1,2,0:T(8,128)S(1)} %fusion.206, f32[12,512]{1,0:T(8,128)S(1)} %get-tuple-element.454, f32[12,512]{1,0:T(8,128)S(1)} %dynamic-slice_bitcast_fusion.14, pred[512,512]{0,1:T(8,128)(4,1)S(1)} %broadcast_compare_fusion.5), kind=kLoop, calls=%fused_computation.23.clone.1 | loop fusion | flops 18874368 | bytes 31768576 | tf_op jit(solution)/shard_map/while/body/eval_jaxpr/convert_element_type | solution.py:87
  420.7 13.1 %reshape.561 = f32[4,2,96,2,1536]{4,3,2,1,0:T(2,128)} reshape(f32[768,3072]{1,0:T(8,128)} %fusion.137) | data formatting | bytes 18874368 | tf_op jit(solution)/shard_map/reshape | solution.py:373
  433.8 8.1 %constant_dynamic-slice_fusion.5 = bf16[4,2,96,1,1536]{4,3,2,1,0:T(2,128)(2,1)S(1)} fusion(f32[4,2,96,2,1536]{4,3,2,1,0:T(2,128)} %reshape.561, s32[]{:T(128)S(6)} %select_n.254), kind=kLoop, calls=%fused_computation.259 | loop fusion | bytes 4718596 | tf_op jit(solution)/shard_map/jit(dynamic_index_in_dim)/dynamic_slice | solution.py:146
  478.4 7.4 %collective-permute-done.25 = bf16[2,4,96,768]{3,2,1,0:T(8,128)(2,1)} collective-permute-done((bf16[2,4,96,768]{3,2,1,0:T(8,128)(2,1)S(1)}, bf16[2,4,96,768]{3,2,1,0:T(8,128)(2,1)}, u32[]{:S(2)}, u32[]{:S(2)}) %collective-permute-start.25) | collective-permute-done | bytes 1179680 | tf_op jit(solution)/shard_map/ppermute | solution.py:115
  489.1 10.8 %collective-permute-done.34 = bf16[4,2,96,768]{3,2,1,0:T(8,128)(2,1)S(1)} collective-permute-done((bf16[4,2,96,768]{3,2,1,0:T(8,128)(2,1)S(1)}, bf16[4,2,96,768]{3,2,1,0:T(8,128)(2,1)S(1)}, u32[]{:S(2)}, u32[]{:S(2)}) %collective-permute-start.34) | collective-permute-done | bytes 1179680 | tf_op jit(solution)/shard_map/ppermute | solution.py:115
  501.6 9.4 %collective-permute-done.40 = bf16[4,2,96,768]{3,2,0,1:T(8,128)(2,1)S(1)} collective-permute-done((bf16[4,2,96,768]{3,2,0,1:T(8,128)(2,1)S(1)}, bf16[4,2,96,768]{3,2,0,1:T(8,128)(2,1)S(1)}, u32[]{:S(2)}, u32[]{:S(2)}) %collective-permute-start.40) | collective-permute-done | bytes 1179680 | tf_op jit(solution)/shard_map/ppermute | solution.py:115
  515.2 7.0 %collective-permute-done.35 = bf16[4,96,768]{2,1,0:T(8,128)(2,1)S(1)} collective-permute-done((bf16[4,96,768]{2,1,0:T(8,128)(2,1)S(1)}, bf16[4,96,768]{2,1,0:T(8,128)(2,1)S(1)}, u32[]{:S(2)}, u32[]{:S(2)}) %collective-permute-start.35) | collective-permute-done | bytes 589856 | tf_op jit(solution)/shard_map/ppermute | solution.py:115
  530.8 7.2 %collective-permute-done.37 = bf16[96,768]{1,0:T(8,128)(2,1)S(1)} collective-permute-done((bf16[96,768]{1,0:T(8,128)(2,1)S(1)}, bf16[96,768]{1,0:T(8,128)(2,1)S(1)}, u32[]{:S(2)}, u32[]{:S(2)}) %collective-permute-start.37) | collective-permute-done | bytes 147488 | tf_op jit(solution)/shard_map/ppermute | solution.py:115
  542.0 10.4 %collective-permute-done.43 = bf16[96,768]{1,0:T(8,128)(2,1)S(1)} collective-permute-done((bf16[96,768]{1,0:T(8,128)(2,1)S(1)}, bf16[96,768]{1,0:T(8,128)(2,1)S(1)}, u32[]{:S(2)}, u32[]{:S(2)}) %collective-permute-start.43) | collective-permute-done | bytes 147488 | tf_op jit(solution)/shard_map/ppermute | solution.py:115
  554.5 8.4 %collective-permute-done.45 = bf16[3,96,768]{2,1,0:T(8,128)(2,1)S(1)} collective-permute-done((bf16[3,96,768]{2,1,0:T(8,128)(2,1)S(1)}, bf16[3,96,768]{2,1,0:T(8,128)(2,1)S(1)}, u32[]{:S(2)}, u32[]{:S(2)}) %collective-permute-start.45) | collective-permute-done | bytes 442400 | tf_op jit(solution)/shard_map/ppermute | solution.py:115
  564.8 16.9 %collective-permute-done.46 = bf16[3,2,96,768]{3,2,1,0:T(8,128)(2,1)S(1)} collective-permute-done((bf16[3,2,96,768]{3,2,1,0:T(8,128)(2,1)S(1)}, bf16[3,2,96,768]{3,2,1,0:T(8,128)(2,1)S(1)}, u32[]{:S(2)}, u32[]{:S(2)}) %collective-permute-start.46) | collective-permute-done | bytes 884768 | tf_op jit(solution)/shard_map/ppermute | solution.py:115
  (541 shorter events, 359.1 us)
Async XLA Ops:
  6.2 26.6 %collective-permute-start.13 = (bf16[96,768]{1,0:T(8,128)(2,1)S(1)}, bf16[96,768]{1,0:T(8,128)(2,1)S(1)}, u32[]{:S(2)}, u32[]{:S(2)}) collective-permute-start(bf16[96,768]{1,0:T(8,128)(2,1)S(1)} %get-tuple-element.290), channel_id=1, source_target_pairs={{0,2},{1,3},{2,0},{3,1},{4,6},{5,7},{6,4},{7,5},{8,10},{9,11},{10,... | collective-permute-start | bytes 442376 | tf_op jit(solution)/shard_map/ppermute | solution.py:115
  8.8 24.7 %collective-permute-start.14 = (bf16[96,768]{1,0:T(8,128)(2,1)S(1)}, bf16[96,768]{1,0:T(8,128)(2,1)S(1)}, u32[]{:S(2)}, u32[]{:S(2)}) collective-permute-start(bf16[96,768]{1,0:T(8,128)(2,1)S(1)} %get-tuple-element.290), channel_id=1, source_target_pairs={{0,3},{1,2},{2,1},{3,0},{4,7},{5,6},{6,5},{7,4},{8,11},{9,10},{10,... | collective-permute-start | bytes 442376 | tf_op jit(solution)/shard_map/ppermute | solution.py:115
  16.3 54.2 %collective-permute-start = (bf16[99,768]{1,0:T(8,128)(2,1)S(1)}, bf16[99,768]{1,0:T(8,128)(2,1)S(1)}, u32[]{:S(2)}, u32[]{:S(2)}) collective-permute-start(bf16[99,768]{1,0:T(8,128)(2,1)S(1)} %pad_maximum_fusion.3), channel_id=1, source_target_pairs={{0,1},{1,0},{2,3},{3,2},{4,5},{5,4},{6,7},{7,6},{8,9},{9,8},{10,11... | collective-permute-start | bytes 456200 | tf_op jit(solution)/shard_map/ppermute | solution.py:115
  17.3 53.3 %collective-permute-start.1 = (bf16[99,768]{1,0:T(8,128)(2,1)S(1)}, bf16[99,768]{1,0:T(8,128)(2,1)S(1)}, u32[]{:S(2)}, u32[]{:S(2)}) collective-permute-start(bf16[99,768]{1,0:T(8,128)(2,1)S(1)} %pad_maximum_fusion.3), channel_id=1, source_target_pairs={{0,2},{1,3},{2,0},{3,1},{4,6},{5,7},{6,4},{7,5},{8,10},{9,11},{10,... | collective-permute-start | bytes 456200 | tf_op jit(solution)/shard_map/ppermute | solution.py:115
  30.1 40.5 %collective-permute-start.2 = (bf16[99,768]{1,0:T(8,128)(2,1)S(1)}, bf16[99,768]{1,0:T(8,128)(2,1)}, u32[]{:S(2)}, u32[]{:S(2)}) collective-permute-start(bf16[99,768]{1,0:T(8,128)(2,1)S(1)} %pad_maximum_fusion.3), channel_id=1, source_target_pairs={{0,3},{1,2},{2,1},{3,0},{4,7},{5,6},{6,5},{7,4},{8,11},{9,10},{10,... | collective-permute-start | bytes 456200 | tf_op jit(solution)/shard_map/ppermute | solution.py:115
  48.5 24.6 %collective-permute-start.15 = (bf16[4,96,768]{2,1,0:T(8,128)(2,1)}, bf16[4,96,768]{2,1,0:T(8,128)(2,1)}, u32[]{:S(2)}, u32[]{:S(2)}) collective-permute-start(bf16[4,96,768]{2,1,0:T(8,128)(2,1)} %bitcast_dynamic-update-slice_fusion.24), channel_id=1, source_target_pairs={{0,4},{4,0},{8,12},{12,8},{1,5},{5,1},{9,13},{13,9},{2,6},{6,2},{1... | collective-permute-start | bytes 1769480 | tf_op jit(solution)/shard_map/ppermute | solution.py:115
  51.3 24.2 %collective-permute-start.9 = (bf16[4,96,768]{2,1,0:T(8,128)(2,1)}, bf16[4,96,768]{2,1,0:T(8,128)(2,1)}, u32[]{:S(2)}, u32[]{:S(2)}) collective-permute-start(bf16[4,96,768]{2,1,0:T(8,128)(2,1)} %bitcast_dynamic-update-slice_fusion.28), channel_id=1, source_target_pairs={{0,8},{4,12},{8,0},{12,4},{1,9},{5,13},{9,1},{13,5},{2,10},{6,14},... | collective-permute-start | bytes 1769480 | tf_op jit(solution)/shard_map/ppermute | solution.py:115
  72.4 30.8 %collective-permute-start.3 = (bf16[4,96,768]{2,1,0:T(8,128)(2,1)}, bf16[4,96,768]{2,1,0:T(8,128)(2,1)}, u32[]{:S(2)}, u32[]{:S(2)}) collective-permute-start(bf16[4,96,768]{2,1,0:T(8,128)(2,1)} %slice.156), channel_id=1, source_target_pairs={{0,4},{4,0},{8,12},{12,8},{1,5},{5,1},{9,13},{13,9},{2,6},{6,2},{1... | collective-permute-start | bytes 1769480 | tf_op jit(solution)/shard_map/ppermute | solution.py:115
  100.9 29.0 %collective-permute-start.16 = (bf16[4,2,96,768]{3,2,1,0:T(8,128)(2,1)}, bf16[4,2,96,768]{3,2,1,0:T(8,128)(2,1)S(1)}, u32[]{:S(2)}, u32[]{:S(2)}) collective-permute-start(bf16[4,2,96,768]{3,2,1,0:T(8,128)(2,1)} %bitcast_dynamic-update-slice_fusion.17), channel_id=1, source_target_pairs={{0,8},{4,12},{8,0},{12,4},{1,9},{5,13},{9,1},{13,5},{2,10},{6,14},... | collective-permute-start | bytes 3538952 | tf_op jit(solution)/shard_map/ppermute | solution.py:115
  101.4 24.6 %collective-permute-start.10 = (bf16[4,96,1536]{2,1,0:T(8,128)(2,1)}, bf16[4,96,1536]{2,1,0:T(8,128)(2,1)S(1)}, u32[]{:S(2)}, u32[]{:S(2)}) collective-permute-start(bf16[4,96,1536]{2,1,0:T(8,128)(2,1)} %reshape.542), channel_id=1, source_target_pairs={{0,4},{4,0},{8,12},{12,8},{1,5},{5,1},{9,13},{13,9},{2,6},{6,2},{1... | collective-permute-start | bytes 3538952 | tf_op jit(solution)/shard_map/ppermute | solution.py:115
  104.3 46.7 %collective-permute-start.4 = (bf16[4,2,96,768]{3,2,1,0:T(8,128)(2,1)S(1)}, bf16[4,2,96,768]{3,2,1,0:T(8,128)(2,1)S(1)}, u32[]{:S(2)}, u32[]{:S(2)}) collective-permute-start(bf16[4,2,96,768]{3,2,1,0:T(8,128)(2,1)S(1)} %bitcast_dynamic-update-slice_fusion.18), channel_id=1, source_target_pairs={{0,8},{4,12},{8,0},{12,4},{1,9},{5,13},{9,1},{13,5},{2,10},{6,14},... | collective-permute-start | bytes 3538952 | tf_op jit(solution)/shard_map/ppermute | solution.py:115
  126.1 44.7 %collective-permute-start.11 = (bf16[768,1536]{1,0:T(8,128)(2,1)S(1)}, bf16[768,1536]{1,0:T(8,128)(2,1)}, u32[]{:S(2)}, u32[]{:S(2)}) collective-permute-start(bf16[768,1536]{1,0:T(8,128)(2,1)S(1)} %bitcast.479), channel_id=1, source_target_pairs={{0,16},{16,0},{1,17},{17,1},{2,18},{18,2},{3,19},{19,3},{4,20},{20... | collective-permute-start | bytes 7077896 | tf_op jit(solution)/shard_map/ppermute | solution.py:115
  131.0 46.5 %collective-permute-start.17 = (bf16[4,2,2,96,768]{4,3,2,1,0:T(8,128)(2,1)}, bf16[4,2,2,96,768]{4,3,2,1,0:T(8,128)(2,1)}, u32[]{:S(2)}, u32[]{:S(2)}) collective-permute-start(bf16[4,2,2,96,768]{4,3,2,1,0:T(8,128)(2,1)} %bitcast_dynamic-update-slice_fusion.7), channel_id=1, source_target_pairs={{0,16},{16,0},{1,17},{17,1},{2,18},{18,2},{3,19},{19,3},{4,20},{20... | collective-permute-start | bytes 7077896 | tf_op jit(solution)/shard_map/ppermute | solution.py:115
  152.1 29.3 %collective-permute-start.5 = (bf16[2,4,2,96,768]{4,3,2,1,0:T(8,128)(2,1)}, bf16[2,4,2,96,768]{4,3,2,1,0:T(8,128)(2,1)}, u32[]{:S(2)}, u32[]{:S(2)}) collective-permute-start(bf16[2,4,2,96,768]{4,3,2,1,0:T(8,128)(2,1)} %bitcast_dynamic-update-slice_fusion.11), channel_id=1, source_target_pairs={{0,16},{16,0},{1,17},{17,1},{2,18},{18,2},{3,19},{19,3},{4,20},{20... | collective-permute-start | bytes 7077896 | tf_op jit(solution)/shard_map/ppermute | solution.py:115
  405.0 42.6 %collective-permute-start.27 = (bf16[4,2304]{1,0:T(4,128)(2,1)S(1)}, bf16[4,2304]{1,0:T(4,128)(2,1)S(1)}, u32[]{:S(2)}, u32[]{:S(2)}) collective-permute-start(bf16[4,2304]{1,0:T(4,128)(2,1)S(1)} %constant_dynamic-update-slice_fusion.8), channel_id=1, source_target_pairs={{0,16},{16,0},{1,17},{17,1},{2,18},{18,2},{3,19},{19,3},{4,20},{20... | collective-permute-start | bytes 55304 | tf_op jit(solution)/shard_map/ppermute | solution.py:115
  420.2 34.2 %collective-permute-start.24 = (bf16[2,4,2,96,768]{4,3,1,0,2:T(8,128)(2,1)S(1)}, bf16[2,4,2,96,768]{4,3,1,0,2:T(8,128)(2,1)}, u32[]{:S(2)}, u32[]{:S(2)}) collective-permute-start(bf16[2,4,2,96,768]{4,3,1,0,2:T(8,128)(2,1)S(1)} %fusion.68), channel_id=1, source_target_pairs={{0,16},{16,0},{1,17},{17,1},{2,18},{18,2},{3,19},{19,3},{4,20},{20... | collective-permute-start | bytes 7077896 | tf_op jit(solution)/shard_map/ppermute | solution.py:115
  447.1 25.5 %collective-permute-start.39 = (bf16[4,2,2,96,768]{4,3,0,1,2:T(8,128)(2,1)}, bf16[4,2,2,96,768]{4,3,0,1,2:T(8,128)(2,1)}, u32[]{:S(2)}, u32[]{:S(2)}) collective-permute-start(bf16[4,2,2,96,768]{4,3,0,1,2:T(8,128)(2,1)} %fusion.70), channel_id=1, source_target_pairs={{0,16},{16,0},{1,17},{17,1},{2,18},{18,2},{3,19},{19,3},{4,20},{20... | collective-permute-start | bytes 7077896 | tf_op jit(solution)/shard_map/ppermute | solution.py:115
  453.9 23.8 %collective-permute-start.29 = (bf16[4,2304]{1,0:T(4,128)(2,1)}, bf16[4,2304]{1,0:T(4,128)(2,1)}, u32[]{:S(2)}, u32[]{:S(2)}) collective-permute-start(bf16[4,2304]{1,0:T(4,128)(2,1)} %add_convert_fusion.4), channel_id=1, source_target_pairs={{0,8},{4,12},{8,0},{12,4},{1,9},{5,13},{9,1},{13,5},{2,10},{6,14},... | collective-permute-start | bytes 55304 | tf_op jit(solution)/shard_map/ppermute | solution.py:115
  456.8 29.0 %collective-permute-start.25 = (bf16[2,4,96,768]{3,2,1,0:T(8,128)(2,1)S(1)}, bf16[2,4,96,768]{3,2,1,0:T(8,128)(2,1)}, u32[]{:S(2)}, u32[]{:S(2)}) collective-permute-start(bf16[2,4,96,768]{3,2,1,0:T(8,128)(2,1)S(1)} %dynamic-slice_bitcast_fusion.2), channel_id=1, source_target_pairs={{0,4},{4,0},{8,12},{12,8},{1,5},{5,1},{9,13},{13,9},{2,6},{6,2},{1... | collective-permute-start | bytes 3538952 | tf_op jit(solution)/shard_map/ppermute | solution.py:115
  471.0 28.9 %collective-permute-start.34 = (bf16[4,2,96,768]{3,2,1,0:T(8,128)(2,1)S(1)}, bf16[4,2,96,768]{3,2,1,0:T(8,128)(2,1)S(1)}, u32[]{:S(2)}, u32[]{:S(2)}) collective-permute-start(bf16[4,2,96,768]{3,2,1,0:T(8,128)(2,1)S(1)} %bitcast.530), channel_id=1, source_target_pairs={{0,8},{4,12},{8,0},{12,4},{1,9},{5,13},{9,1},{13,5},{2,10},{6,14},... | collective-permute-start | bytes 3538952 | tf_op jit(solution)/shard_map/ppermute | solution.py:115
  476.4 34.6 %collective-permute-start.40 = (bf16[4,2,96,768]{3,2,0,1:T(8,128)(2,1)S(1)}, bf16[4,2,96,768]{3,2,0,1:T(8,128)(2,1)S(1)}, u32[]{:S(2)}, u32[]{:S(2)}) collective-permute-start(bf16[4,2,96,768]{3,2,0,1:T(8,128)(2,1)S(1)} %dynamic-slice_bitcast_fusion.1), channel_id=1, source_target_pairs={{0,4},{4,0},{8,12},{12,8},{1,5},{5,1},{9,13},{13,9},{2,6},{6,2},{1... | collective-permute-start | bytes 3538952 | tf_op jit(solution)/shard_map/ppermute | solution.py:115
  487.5 25.5 %collective-permute-start.26 = (bf16[4,96,768]{2,1,0:T(8,128)(2,1)S(1)}, bf16[4,96,768]{2,1,0:T(8,128)(2,1)S(1)}, u32[]{:S(2)}, u32[]{:S(2)}) collective-permute-start(bf16[4,96,768]{2,1,0:T(8,128)(2,1)S(1)} %dynamic-slice_bitcast_fusion.5), channel_id=1, source_target_pairs={{0,8},{4,12},{8,0},{12,4},{1,9},{5,13},{9,1},{13,5},{2,10},{6,14},... | collective-permute-start | bytes 1769480 | tf_op jit(solution)/shard_map/ppermute | solution.py:115
  513.2 39.4 %collective-permute-start.30 = (bf16[99,768]{1,0:T(8,128)(2,1)S(1)}, bf16[99,768]{1,0:T(8,128)(2,1)S(1)}, u32[]{:S(2)}, u32[]{:S(2)}) collective-permute-start(bf16[99,768]{1,0:T(8,128)(2,1)S(1)} %get-tuple-element.306), channel_id=1, source_target_pairs={{0,1},{1,0},{2,3},{3,2},{4,5},{5,4},{6,7},{7,6},{8,9},{9,8},{10,11... | collective-permute-start | bytes 456200 | tf_op jit(solution)/shard_map/ppermute | solution.py:115
  514.8 37.7 %collective-permute-start.31 = (bf16[99,768]{1,0:T(8,128)(2,1)S(1)}, bf16[99,768]{1,0:T(8,128)(2,1)S(1)}, u32[]{:S(2)}, u32[]{:S(2)}) collective-permute-start(bf16[99,768]{1,0:T(8,128)(2,1)S(1)} %get-tuple-element.307), channel_id=1, source_target_pairs={{0,2},{1,3},{2,0},{3,1},{4,6},{5,7},{6,4},{7,5},{8,10},{9,11},{10,... | collective-permute-start | bytes 456200 | tf_op jit(solution)/shard_map/ppermute | solution.py:115
  (122 other events, 940.8 us)
